TPU v7x, 256 devices: a whole 4x4x8 slice. The times are simulated.
256 devices in a mesh: dp: 2 (over y_hi), fsdp: 16 (over x, y_lo, core), tensor: 8 (over z).
Axes of the slice: x: 4, y: 4 (y_hi: 2, y_lo: 2; y = y_hi * 2 + y_lo), z: 8, core: 2. Of those that a mesh axis runs over, the one named last changes fastest.
Arguments:
- activations: bfloat16 [4096, 8192], P(('dp', 'fsdp'), 'tensor'), may hold values from -6 to 6
- cotangent: bfloat16 [4096, 8192], P(('dp', 'fsdp'), 'tensor'), may hold values from -6 to 6
- up_tiles: bfloat16 [1024, 128, 128], P(('fsdp', 'tensor')), may hold values from -0.1875 to 0.1875
- down_tiles: bfloat16 [1024, 128, 128], P(('fsdp', 'tensor')), may hold values from -0.125 to 0.125
- up_rows: int32 [128, 8], P(None, 'tensor'), may hold values from 0 to 63, as said below
- up_cols: int32 [128, 8], P(None, 'tensor'), may hold values from 0 to 15, as said below
- down_rows: int32 [128, 8], P(None, 'tensor'), may hold values from 0 to 15, as said below
- down_cols: int32 [128, 8], P(None, 'tensor'), may hold values from 0 to 63, as said below
Outputs:
- output: bfloat16 [4096, 8192], P(('dp', 'fsdp'), 'tensor')
- input_grad: bfloat16 [4096, 8192], P(('dp', 'fsdp'), 'tensor')
- up_grad: float32 [1024, 128, 128], P(('fsdp', 'tensor'))
- down_grad: float32 [1024, 128, 128], P(('fsdp', 'tensor'))
Inputs may be any that keep to these rules, and one draw needn't show every extreme that they name: `up_rows`: within a column, the up tiles of one hidden-unit block name distinct feature blocks. `up_cols`: every value occurs exactly 8 times in each column. `down_rows`: every value occurs exactly 8 times in each column. `down_cols`: within a column, the down tiles of one hidden-unit block name distinct feature blocks.
All inputs are finite; a program needn't handle non-finite values.
Results may differ from a plain program's by a relative error of at most 0.018.
Values may be sent and summed in bfloat16 or wider, within the bound.
No kernel may reach another device: no remote copies, remote signals or barrier semaphores. Data moves between devices by JAX's collectives and lax.ppermute only.
A program may use at most 128 MiB of HBM per device.

v0:
```python
import jax
import jax.numpy as jnp
from jax import lax
from jax.sharding import PartitionSpec as P

D = 8192
FF = 16384
inv_root_two = 0.7071067811865476
inv_root_tau = 0.3989422804014327


def gelu_parts(values):
    normal_cdf = 0.5 * (1.0 + jax.scipy.special.erf(values * inv_root_two))
    density = inv_root_tau * jnp.exp(-0.5 * values * values)
    return (values * normal_cdf, normal_cdf + values * density)


def grouped_pick(acting, far_index, hidden_blocks, block_size):
    rows_here = acting.shape[0]
    picked = acting.reshape(rows_here, -1, block_size)[:, far_index]
    return picked.reshape(rows_here, hidden_blocks, -1, block_size)


def add_far(product, far_index, model_blocks):
    rows_here = product.shape[0]
    block_size = product.shape[-1]
    flat = product.reshape(rows_here, -1, block_size)
    summed = (
        jnp.zeros((rows_here, model_blocks, block_size), jnp.float32).at[:, far_index].add(flat)
    )
    return summed.reshape(rows_here, model_blocks * block_size)


def grouped_tiles(tiles, order, hidden_blocks):
    block_size = tiles.shape[1]
    return tiles[order].reshape(hidden_blocks, -1, block_size, block_size)


def body(activations, cotangent, up_tiles, down_tiles, up_rows, up_cols, down_rows, down_cols):
    block_size = up_tiles.shape[1]
    hidden_blocks = FF // (block_size * lax.axis_size("tensor"))
    model_blocks = D // block_size
    up_order = jnp.argsort(up_cols[:, 0], stable=True)
    down_order = jnp.argsort(down_rows[:, 0], stable=True)
    up_back = jnp.argsort(up_order)
    down_back = jnp.argsort(down_order)
    up_far = up_rows[:, 0][up_order]
    down_far = down_cols[:, 0][down_order]
    full_input = lax.all_gather(activations, "tensor", axis=1, tiled=True)
    input_pick = grouped_pick(full_input, up_far, hidden_blocks, block_size)
    up_whole = lax.all_gather(up_tiles, "fsdp", axis=0, tiled=True)
    up_sorted = grouped_tiles(up_whole, up_order, hidden_blocks)
    pre_act = jnp.einsum(
        "thkb,hkbc->thc", input_pick, up_sorted, preferred_element_type=jnp.float32
    )
    gelu_out, gelu_slope = gelu_parts(pre_act)
    hidden = gelu_out.astype(jnp.bfloat16)
    down_whole = lax.all_gather(down_tiles, "fsdp", axis=0, tiled=True)
    down_sorted = grouped_tiles(down_whole, down_order, hidden_blocks)
    out_product = jnp.einsum(
        "thb,hkbc->thkc", hidden, down_sorted, preferred_element_type=jnp.float32
    )
    partial_out = add_far(out_product, down_far, model_blocks)
    output = lax.psum_scatter(
        partial_out.astype(jnp.bfloat16), "tensor", scatter_dimension=1, tiled=True
    )
    full_cotangent = lax.all_gather(cotangent, "tensor", axis=1, tiled=True)
    cot_pick = grouped_pick(full_cotangent, down_far, hidden_blocks, block_size)
    hidden_grad = jnp.einsum(
        "thkc,hkbc->thb", cot_pick, down_sorted, preferred_element_type=jnp.float32
    )
    pre_grad = (hidden_grad * gelu_slope).astype(jnp.bfloat16)
    in_product = jnp.einsum(
        "thc,hkbc->thkb", pre_grad, up_sorted, preferred_element_type=jnp.float32
    )
    partial_in = add_far(in_product, up_far, model_blocks)
    input_grad = lax.psum_scatter(
        partial_in.astype(jnp.bfloat16), "tensor", scatter_dimension=1, tiled=True
    )
    up_grouped = jnp.einsum(
        "thkb,thc->hkbc", input_pick, pre_grad, preferred_element_type=jnp.float32
    )
    down_grouped = jnp.einsum(
        "thb,thkc->hkbc", hidden, cot_pick, preferred_element_type=jnp.float32
    )
    up_rounded = up_grouped.astype(jnp.bfloat16).reshape(-1, block_size, block_size)
    down_rounded = down_grouped.astype(jnp.bfloat16).reshape(-1, block_size, block_size)
    up_term = up_rounded[up_back].astype(jnp.float32)
    down_term = down_rounded[down_back].astype(jnp.float32)
    up_part, down_part = (
        lax.psum_scatter(
            up_term.astype(jnp.bfloat16), "fsdp", scatter_dimension=0, tiled=True
        ).astype(jnp.float32),
        lax.psum_scatter(
            down_term.astype(jnp.bfloat16), "fsdp", scatter_dimension=0, tiled=True
        ).astype(jnp.float32),
    )
    up_grad, down_grad = (
        lax.psum(up_part.astype(jnp.bfloat16), "dp").astype(jnp.float32),
        lax.psum(down_part.astype(jnp.bfloat16), "dp").astype(jnp.float32),
    )
    return (output, input_grad, up_grad, down_grad)


def solution(mesh):
    in_specs = (
        P(("dp", "fsdp"), "tensor"),
        P(("dp", "fsdp"), "tensor"),
        P(("fsdp", "tensor"), None, None),
        P(("fsdp", "tensor"), None, None),
        P(None, "tensor"),
        P(None, "tensor"),
        P(None, "tensor"),
        P(None, "tensor"),
    )
    out_specs = (
        P(("dp", "fsdp"), "tensor"),
        P(("dp", "fsdp"), "tensor"),
        P(("fsdp", "tensor"), None, None),
        P(("fsdp", "tensor"), None, None),
    )
    return jax.shard_map(body, mesh=mesh, in_specs=in_specs, out_specs=out_specs, check_vma=False)
```

profile of v0, /device:TPU:1, one launch (start us, length us, event | category | flops | bytes accessed | tf_op | source)
XLA Modules:
  0.0 480.6 jit_solution(9236470539080875752)
XLA Ops:
  7.2 0.0 all-gather.9.cloned.1.call-start
  7.2 1.8 copy.58
  9.0 0.0 all-gather.9.cloned.1.call-update
  9.0 0.0 all-gather.11.cloned.1.call-start
  9.1 1.8 copy.65
  10.9 0.0 all-gather.11.cloned.1.call-update
  10.9 0.0 all-gather.7.cloned.1.call-start
  11.0 0.7 all-gather.7.cloned.1.call-update
  11.7 0.0 all-gather.5.cloned.1.call-start
  11.7 0.5 all-gather.5.cloned.1.call-update
  12.2 0.0 reduce-scatter.9.cloned.1.call-start
  12.3 3.2 sort.63
  15.5 2.5 sort.64
  18.0 1.2 gather_fusion.3
  19.3 3.2 sort.62
  22.5 1.6 gather_fusion
  24.1 28.0 %all-gather.9.cloned.1.call-done = bf16[128,8192]{0,1:T(8,128)(2,1)} async-done(((bf16[128,1024]{0,1:T(8,128)(2,1)}), bf16[128,8192]{0,1:T(8,128)(2,1)}) %all-gather.9.cloned.1.call-update) | async-done | bytes 2097168 | tf_op jit(solution)/shard_map/all_gather | solution.py:49
  52.1 3.2 copy.59
  55.3 39.0 %all-gather.11.cloned.1.call-done = bf16[128,8192]{0,1:T(8,128)(2,1)} async-done(((bf16[128,1024]{0,1:T(8,128)(2,1)}), bf16[128,8192]{0,1:T(8,128)(2,1)}) %all-gather.11.cloned.1.call-update) | async-done | bytes 2097168 | tf_op jit(solution)/shard_map/all_gather | solution.py:67
  94.3 4.1 copy.66
  98.4 3.0 gather_fusion.4
  101.4 4.6 gather_fusion.5
  106.0 32.7 %all-gather.7.cloned.1.call-done = bf16[128,128,128]{2,1,0:T(8,128)(2,1)} async-done(((bf16[8,128,128]{2,1,0:T(8,128)(2,1)}), bf16[128,128,128]{2,1,0:T(8,128)(2,1)}) %all-gather.7.cloned.1.call-update) | async-done | bytes 4194320 | tf_op jit(solution)/shard_map/all_gather | solution.py:51
  138.7 5.2 %gather_fusion.2 = bf16[128,128,128]{2,1,0:T(8,128)(2,1)} fusion(bf16[128,128,128]{2,1,0:T(8,128)(2,1)} %all-gather.7.cloned.1.call-done, s32[1024]{0:T(1024)S(1)} %pad_clamp_fusion.4), kind=kCustom, calls=%fused_computation.2 | custom fusion | bytes 8389120 | tf_op jit(solution)/shard_map/gather | solution.py:36
  143.9 4.8 convolution_bitcast_fusion.1
  148.7 31.7 %all-gather.5.cloned.1.call-done = bf16[128,128,128]{2,1,0:T(8,128)(2,1)} async-done(((bf16[8,128,128]{2,1,0:T(8,128)(2,1)}), bf16[128,128,128]{2,1,0:T(8,128)(2,1)}) %all-gather.5.cloned.1.call-update) | async-done | bytes 4194320 | tf_op jit(solution)/shard_map/all_gather | solution.py:58
  180.5 5.2 %gather_fusion.1 = bf16[128,128,128]{2,1,0:T(8,128)(2,1)} fusion(bf16[128,128,128]{2,1,0:T(8,128)(2,1)} %all-gather.5.cloned.1.call-done, s32[1024]{0:T(1024)S(1)} %pad_clamp_fusion.5), kind=kCustom, calls=%fused_computation.1 | custom fusion | bytes 8389120 | tf_op jit(solution)/shard_map/gather | solution.py:36
  185.7 5.0 %fusion.2 = bf16[128,16,128,1]{0,2,3,1:T(8,128)(2,1)S(1)} fusion(bf16[16,8,128,128]{3,2,1,0:T(8,128)(2,1)} %bitcast.84, bf16[128,16,8,128]{3,0,2,1:T(8,128)(2,1)} %bitcast.86, f32[128,16,128]{0,2,1:T(8,128)S(1)} %convolution_bitcast_fusion.1), kind=kOutput, calls=%fused_computation.17 | convolution fusion | flops 539492352 | bytes 9961472 | tf_op jit(solution)/shard_map/thkc,hkbc->thb/dot_general | solution.py:69
  190.7 3.3 convolution_convert_fusion.1
  194.0 5.2 %gather_fusion.6 = bf16[128,128,128]{2,1,0:T(8,128)(2,1)} fusion(bf16[128,128,128]{2,1,0:T(8,128)(2,1)} %bitcast.88, s32[1024]{0:T(1024)S(1)} %pad_clamp_fusion.1), kind=kCustom, calls=%fused_computation.6 | custom fusion | bytes 8389120 | tf_op jit(solution)/shard_map/gather | solution.py:88
  199.2 0.0 reduce-scatter.9.cloned.1.call-update
  199.2 0.2 reduce-scatter.11.cloned.1.call-start
  199.5 2.5 sort.65
  202.0 5.6 %convolution_convert_fusion = bf16[16,8,128,128]{3,2,1,0:T(8,128)(2,1)} fusion(bf16[128,16,8,128]{3,0,2,1:T(8,128)(2,1)} %bitcast.87, f32[128,16,128]{0,2,1:T(8,128)S(1)} %convolution_bitcast_fusion.1), kind=kOutput, calls=%fused_computation.10 | convolution fusion | flops 540278784 | bytes 9437184 | tf_op jit(solution)/shard_map/thb,thkc->hkbc/dot_general | solution.py:83
  207.6 6.4 %copy.74 = bf16[128,128,128]{2,1,0:T(8,128)(2,1)} copy(bf16[128,128,128]{1,2,0:T(8,128)(2,1)} %bitcast.89) | data formatting | bytes 8388608 | tf_op jit(solution)/shard_map/reshape | solution.py:87
  214.0 5.3 %gather_fusion.7 = bf16[128,128,128]{2,1,0:T(8,128)(2,1)} fusion(bf16[128,128,128]{2,1,0:T(8,128)(2,1)} %copy.74, s32[1024]{0:T(1024)S(1)} %pad_clamp_fusion), kind=kCustom, calls=%fused_computation.7 | custom fusion | bytes 8389120 | tf_op jit(solution)/shard_map/gather | solution.py:89
  219.3 0.0 reduce-scatter.11.cloned.1.call-update
  219.4 0.0 reduce-scatter.7.cloned.1.call-start
  219.4 6.7 %fusion.13 = f32[16,8,128,128]{3,2,1,0:T(8,128)} fusion(bf16[16,8,128,128]{3,2,1,0:T(8,128)(2,1)} %bitcast.77, bf16[128,16,128,1]{0,2,3,1:T(8,128)(2,1)S(1)} %fusion.2), kind=kOutput, calls=%fused_computation.40 | convolution fusion | flops 536870912 | bytes 13107200 | tf_op jit(solution)/shard_map/thc,hkbc->thkb/dot_general | solution.py:73
  226.1 9.0 %copy.68 = f32[128,128,128]{2,0,1:T(8,128)} copy(f32[128,128,128]{0,2,1:T(8,128)} %bitcast.82) | data formatting | bytes 16777216 | tf_op jit(solution)/shard_map/reshape | solution.py:27
  235.1 2.5 broadcast.42.clone.1
  237.6 26.7 %scatter_fusion.1 = f32[128,64,128]{2,0,1:T(8,128)} fusion(f32[128,64,128]{2,0,1:T(8,128)} %broadcast.42.clone.1, s32[128]{0:T(128)S(1)} %fusion.9, f32[128,128,128]{2,1,0:T(8,128)} %bitcast.81), kind=kCustom, calls=%fused_computation.9 | custom fusion | flops 2097152 | bytes 25166336 | tf_op jit(solution)/shard_map/scatter-add | solution.py:29
  264.3 2.6 convert_element_type.45
  266.9 2.9 copy.69
  269.9 0.0 reduce-scatter.7.cloned.1.call-update
  269.9 0.0 reduce-scatter.5.cloned.1.call-start
  270.0 6.8 %fusion.11 = f32[16,8,128,128]{3,2,1,0:T(8,128)} fusion(bf16[16,8,128,128]{3,2,1,0:T(8,128)(2,1)} %bitcast.85, f32[128,16,128]{0,2,1:T(8,128)S(1)} %convolution_bitcast_fusion.1), kind=kOutput, calls=%fused_computation.39 | convolution fusion | flops 538181632 | bytes 13631488 | tf_op jit(solution)/shard_map/thb,hkbc->thkc/dot_general | solution.py:60
  276.7 9.0 %copy.63 = f32[128,128,128]{2,0,1:T(8,128)} copy(f32[128,128,128]{0,2,1:T(8,128)} %bitcast.83) | data formatting | bytes 16777216 | tf_op jit(solution)/shard_map/reshape | solution.py:27
  285.8 2.5 broadcast.42.clone
  288.2 26.9 %scatter_fusion = f32[128,64,128]{2,0,1:T(8,128)} fusion(f32[128,64,128]{2,0,1:T(8,128)} %broadcast.42.clone, s32[128]{0:T(128)S(1)} %fusion.8, f32[128,128,128]{2,1,0:T(8,128)} %bitcast.80), kind=kCustom, calls=%fused_computation.8 | custom fusion | flops 2097152 | bytes 25166336 | tf_op jit(solution)/shard_map/scatter-add | solution.py:29
  315.1 2.6 convert_element_type.42
  317.7 2.9 copy.64
  320.6 0.0 reduce-scatter.5.cloned.1.call-update
  320.7 0.0 all-reduce.3.cloned.1.call-start
  320.7 0.0 reduce-scatter.9.cloned.1.call-done
  320.7 16.4 %reduce-scatter.11.cloned.1.call-done = bf16[8,128,128]{2,1,0:T(8,128)(2,1)} async-done(((bf16[128,128,128]{2,1,0:T(8,128)(2,1)}), bf16[8,128,128]{2,1,0:T(8,128)(2,1)}) %reduce-scatter.11.cloned.1.call-update) | async-done | bytes 262160 | tf_op jit(solution)/shard_map/reduce_scatter | solution.py:94
  337.1 0.0 all-reduce.3.cloned.1.call-update
  337.1 42.2 %reduce-scatter.7.cloned.1.call-done = bf16[128,1024]{0,1:T(8,128)(2,1)} async-done(((bf16[128,8192]{0,1:T(8,128)(2,1)}), bf16[128,1024]{0,1:T(8,128)(2,1)}) %reduce-scatter.7.cloned.1.call-update) | async-done | bytes 262160 | tf_op jit(solution)/shard_map/reduce_scatter | solution.py:77
  379.4 1.8 copy.76
  381.1 41.9 %reduce-scatter.5.cloned.1.call-done = bf16[128,1024]{0,1:T(8,128)(2,1)} async-done(((bf16[128,8192]{0,1:T(8,128)(2,1)}), bf16[128,1024]{0,1:T(8,128)(2,1)}) %reduce-scatter.5.cloned.1.call-update) | async-done | bytes 262160 | tf_op jit(solution)/shard_map/reduce_scatter | solution.py:64
  423.0 1.8 copy.75
  424.8 45.7 %all-reduce.3.cloned.1.call-done = (bf16[8,128,128]{2,1,0:T(8,128)(2,1)}, bf16[8,128,128]{2,1,0:T(8,128)(2,1)}) async-done(((bf16[8,128,128]{2,1,0:T(8,128)(2,1)}, bf16[8,128,128]{2,1,0:T(8,128)(2,1)}), (bf16[8,128,128]{2,1,0:T(8,128)(2,1)}, bf16[8,128,128]{2,1,0:T(8,128)(2,1)})) %all-reduce.3.cloned.1.call-update) | async-done | bytes 524304 | tf_op jit(solution)/shard_map/psum | solution.py:99
  470.5 1.8 convert_element_type.48
  472.3 1.8 convert_element_type.51
  (22 shorter events, 0.1 us)
Async XLA Ops:
  7.2 10.9 %copy-start = (s32[128,1]{0,1:T(1,128)S(1)}, s32[128,1]{0,1:T(1,128)}, u32[]{:S(2)}) copy-start(s32[128,1]{0,1:T(1,128)} %param.12) | copy-start | bytes 1540
  7.2 44.9 %all-gather.9.cloned.1.call-start = ((), (), s32[]{:S(2)}) async-start(), calls=%async_computation.6 | async-start | bytes 2359296 | tf_op jit(solution)/shard_map/all_gather | solution.py:49
  9.0 85.3 %all-gather.11.cloned.1.call-start = ((), (), s32[]{:S(2)}) async-start(), calls=%async_computation.8 | async-start | bytes 2359296 | tf_op jit(solution)/shard_map/all_gather | solution.py:67
  10.9 127.8 %all-gather.7.cloned.1.call-start = ((), (), s32[]{:S(2)}) async-start(), calls=%async_computation.5 | async-start | bytes 4456448 | tf_op jit(solution)/shard_map/all_gather | solution.py:51
  11.7 168.8 %all-gather.5.cloned.1.call-start = ((), (), s32[]{:S(2)}) async-start(), calls=%async_computation.4 | async-start | bytes 4456448 | tf_op jit(solution)/shard_map/all_gather | solution.py:58
  12.2 308.5 %reduce-scatter.9.cloned.1.call-start = ((), (), s32[]{:S(2)}) async-start(), calls=%async_computation.10 | async-start | bytes 4456448 | tf_op jit(solution)/shard_map/reduce_scatter | solution.py:91
  185.7 5.0 %copy-start.2 = (bf16[128,128,128]{2,1,0:T(8,128)(2,1)S(1)}, bf16[128,128,128]{2,1,0:T(8,128)(2,1)}, u32[]{:S(2)}) copy-start(bf16[128,128,128]{2,1,0:T(8,128)(2,1)} %gather_fusion.4) | copy-start | bytes 12582916
  199.2 137.9 %reduce-scatter.11.cloned.1.call-start = ((), (), s32[]{:S(2)}) async-start(), calls=%async_computation.11 | async-start | bytes 4456448 | tf_op jit(solution)/shard_map/reduce_scatter | solution.py:94
  219.4 160.0 %reduce-scatter.7.cloned.1.call-start = ((), (), s32[]{:S(2)}) async-start(), calls=%async_computation.9 | async-start | bytes 2359296 | tf_op jit(solution)/shard_map/reduce_scatter | solution.py:77
  269.9 153.1 %reduce-scatter.5.cloned.1.call-start = ((), (), s32[]{:S(2)}) async-start(), calls=%async_computation.7 | async-start | bytes 2359296 | tf_op jit(solution)/shard_map/reduce_scatter | solution.py:64
  315.1 158.9 %copy-start.1 = (s32[128,1]{0,1:T(1,128)S(1)}, s32[128,1]{0,1:T(1,128)}, u32[]{:S(2)}) copy-start(s32[128,1]{0,1:T(1,128)} %param.12) | copy-start | bytes 1540
  320.7 149.9 %all-reduce.3.cloned.1.call-start = ((), (), s32[]{:S(2)}) async-start(), calls=%async_computation.12 | async-start | bytes 1048576 | tf_op jit(solution)/shard_map/psum | solution.py:99
Sparse Core Ops, SparseCore 0:
  10.4 41.6 all-gather.8
  54.5 39.8 all-gather.10
  96.2 42.5 all-gather.6
  140.4 39.9 all-gather.4
  199.3 66.5 reduce-scatter.8
  268.4 68.6 reduce-scatter.10
  339.7 39.6 reduce-scatter.6
  381.9 41.0 reduce-scatter.4
  425.7 44.8 all-reduce.2
where the time goes:
time: 482 us; the launch traced here: 481 us
  waiting for transfers between devices  279 us (58%)
  local copies, waits for them, and re-layouts  81.1 us (17%)
  other arithmetic  73.8 us (15%)
  matrix products  32.2 us (7%)
  between operations  14 us (3%)
    scatter-add x2, other arithmetic, add_far(): jnp.zeros((rows_here, model_blocks, block_size), jnp.float32)  53.6 us
    psum x1, waiting for transfers between devices, body(): lax.psum(up_part.astype(jnp.bfloat16), 'dp').astype(jnp.float32)  45.7 us
    reduce_scatter x1, waiting for transfers between devices, body(): lax.psum_scatter(partial_in.astype(jnp.bfloat16), 'tensor', scatter_dimen...  42.2 us
    reduce_scatter x1, waiting for transfers between devices, body(): lax.psum_scatter(partial_out.astype(jnp.bfloat16), 'tensor', scatter_dime...  41.9 us
    all_gather x1, waiting for transfers between devices, body(): full_cotangent = lax.all_gather(cotangent, 'tensor', axis=1, tiled=True)  39 us
    all_gather x1, waiting for transfers between devices, body(): up_whole = lax.all_gather(up_tiles, 'fsdp', axis=0, tiled=True)  32.7 us
    all_gather x1, waiting for transfers between devices, body(): down_whole = lax.all_gather(down_tiles, 'fsdp', axis=0, tiled=True)  31.7 us
    all_gather x1, waiting for transfers between devices, body(): full_input = lax.all_gather(activations, 'tensor', axis=1, tiled=True)  28 us
  transfers between devices with their start and end apart: 9, of which 8 were waited for; matrix products, arithmetic and copies ran while one was open for 34% of the time, Pallas kernels for 0%

commit v1 on v0

--- a/solution.py
+++ b/solution.py
@@ -46,7 +46,18 @@
     down_back = jnp.argsort(down_order)
     up_far = up_rows[:, 0][up_order]
     down_far = down_cols[:, 0][down_order]
-    full_input = lax.all_gather(activations, "tensor", axis=1, tiled=True)
+    ways = lax.axis_size("tensor")
+    up = [(d, (d + 1) % ways) for d in range(ways)]
+    down = [(d, (d - 1) % ways) for d in range(ways)]
+    earlier, later = ([activations], [activations])
+    for _ in range(ways // 2):
+        earlier.append(lax.ppermute(earlier[-1], "tensor", up))
+    for _ in range((ways - 1) // 2):
+        later.append(lax.ppermute(later[-1], "tensor", down))
+    line = jnp.concatenate([*earlier[::-1], *later[1:]], axis=1)
+    full_input = jnp.roll(
+        line, (lax.axis_index("tensor") - ways // 2) * activations.shape[1], axis=1
+    )
     input_pick = grouped_pick(full_input, up_far, hidden_blocks, block_size)
     up_whole = lax.all_gather(up_tiles, "fsdp", axis=0, tiled=True)
     up_sorted = grouped_tiles(up_whole, up_order, hidden_blocks)

time: 482 us -> 449 us (0.932)
  waiting for transfers between devices: 279 us -> 234 us
  starting transfers between devices: 0.55 us -> 13.3 us
    all_gather x1, waiting for transfers between devices: 39 us -> 0.01 us  [body(): full_cotangent = lax.all_gather(cotangent, 'tensor', axis=1, tiled=True)]
    all_gather x1 -> x0, waiting for transfers between devices: 28 us -> none  [body(): full_input = lax.all_gather(activations, 'tensor', axis=1, tiled=True)]
    ppermute x0 -> x7, waiting for transfers between devices: none -> 24.4 us  [the longest x4 23.7 us: body(): earlier.append(lax.ppermute(earlier[-1], 'tensor', up))]
    ppermute x0 -> x7, starting transfers between devices: none -> 12.7 us  [the longest x3 10.2 us: body(): later.append(lax.ppermute(later[-1], 'tensor', down))]
    all_gather x1, waiting for transfers between devices: 32.7 us -> 27.5 us  [body(): up_whole = lax.all_gather(up_tiles, 'fsdp', axis=0, tiled=True)]
  transfers between devices with their start and end apart: 9 -> 15, of which waited for: 8 -> 11; matrix products, arithmetic and copies ran while one was open for 34% -> 36% of each run, Pallas kernels for 0% -> 0%
where the time goes in v1:
time: 449 us; the launch traced here: 448 us
  waiting for transfers between devices  234 us (52%)
  local copies, waits for them, and re-layouts  79.9 us (18%)
  other arithmetic  73.9 us (16%)
  matrix products  32.2 us (7%)
  between operations  14.5 us (3%)
  starting transfers between devices  13.3 us (3%)
    scatter-add x2, other arithmetic, add_far(): jnp.zeros((rows_here, model_blocks, block_size), jnp.float32)  53.6 us
    psum x1, waiting for transfers between devices, body(): lax.psum(up_part.astype(jnp.bfloat16), 'dp').astype(jnp.float32)  45.9 us
    reduce_scatter x1, waiting for transfers between devices, body(): lax.psum_scatter(partial_in.astype(jnp.bfloat16), 'tensor', scatter_dimen...  42 us
    reduce_scatter x1, waiting for transfers between devices, body(): lax.psum_scatter(partial_out.astype(jnp.bfloat16), 'tensor', scatter_dime...  41.8 us
    all_gather x1, waiting for transfers between devices, body(): down_whole = lax.all_gather(down_tiles, 'fsdp', axis=0, tiled=True)  31.9 us
    all_gather x1, waiting for transfers between devices, body(): up_whole = lax.all_gather(up_tiles, 'fsdp', axis=0, tiled=True)  27.5 us
    ppermute x4, waiting for transfers between devices, body(): earlier.append(lax.ppermute(earlier[-1], 'tensor', up))  23.7 us
    reduce_scatter x1, waiting for transfers between devices, body(): lax.psum_scatter(down_term.astype(jnp.bfloat16), 'fsdp', scatter_dimensio...  18.9 us
  transfers between devices with their start and end apart: 15, of which 11 were waited for; matrix products, arithmetic and copies ran while one was open for 36% of the time, Pallas kernels for 0%

profile of v1, /device:TPU:1, one launch (start us, length us, event | category | flops | bytes accessed | tf_op | source)
XLA Modules:
  0.0 447.6 jit_solution(830618756637810013)
XLA Ops:
  7.2 0.0 all-gather.8.cloned.1.call-start
  7.2 1.8 copy.70
  9.0 0.0 all-gather.6.cloned.1.call-start
  9.1 0.7 all-gather.6.cloned.1.call-update
  9.8 0.0 all-gather.4.cloned.1.call-start
  9.8 0.7 all-gather.4.cloned.1.call-update
  10.5 0.0 reduce-scatter.9.cloned.1.call-start
  10.6 1.1 copy.60
  11.7 2.5 collective-permute-start
  14.2 4.0 collective-permute-start.4
  18.3 3.2 sort.63
  21.5 1.2 gather_fusion.3
  22.7 3.2 sort.62
  26.0 2.5 sort.65
  28.5 1.6 gather_fusion
  30.1 6.4 %collective-permute-done.1 = bf16[128,1024]{0,1:T(8,128)(2,1)S(1)} collective-permute-done((bf16[128,1024]{0,1:T(8,128)(2,1)S(1)}, bf16[128,1024]{0,1:T(8,128)(2,1)S(1)}, u32[]{:S(2)}, u32[]{:S(2)}) %collective-permute-start.1) | collective-permute-done | bytes 262176 | tf_op jit(solution)/shard_map/ppermute | solution.py:54
  36.5 2.5 sort.64
  39.1 2.7 collective-permute-start.5
  41.7 7.9 %collective-permute-done.2 = bf16[128,1024]{0,1:T(8,128)(2,1)S(1)} collective-permute-done((bf16[128,1024]{0,1:T(8,128)(2,1)S(1)}, bf16[128,1024]{0,1:T(8,128)(2,1)S(1)}, u32[]{:S(2)}, u32[]{:S(2)}) %collective-permute-start.2) | collective-permute-done | bytes 262176 | tf_op jit(solution)/shard_map/ppermute | solution.py:54
  49.7 0.6 collective-permute-done.5
  50.4 3.5 collective-permute-start.6
  53.9 9.3 %collective-permute-done.3 = bf16[128,1024]{0,1:T(8,128)(2,1)S(1)} collective-permute-done((bf16[128,1024]{0,1:T(8,128)(2,1)S(1)}, bf16[128,1024]{0,1:T(8,128)(2,1)S(1)}, u32[]{:S(2)}, u32[]{:S(2)}) %collective-permute-start.3) | collective-permute-done | bytes 262176 | tf_op jit(solution)/shard_map/ppermute | solution.py:54
  63.5 0.1 collective-permute-done.6
  63.9 1.4 constant_dynamic-slice_fusion
  65.4 3.2 copy.64
  68.6 3.0 gather_fusion.4
  71.6 3.2 copy.71
  74.8 3.1 gather_fusion.5
  77.9 27.5 %all-gather.6.cloned.1.call-done = bf16[128,128,128]{2,1,0:T(8,128)(2,1)} async-done(((bf16[8,128,128]{2,1,0:T(8,128)(2,1)}), bf16[128,128,128]{2,1,0:T(8,128)(2,1)}) %all-gather.6.cloned.1.call-update) | async-done | bytes 4194320 | tf_op jit(solution)/shard_map/all_gather | solution.py:62
  105.3 5.2 %gather_fusion.2 = bf16[128,128,128]{2,1,0:T(8,128)(2,1)} fusion(bf16[128,128,128]{2,1,0:T(8,128)(2,1)} %all-gather.6.cloned.1.call-done, s32[1024]{0:T(1024)S(1)} %pad_clamp_fusion.4), kind=kCustom, calls=%fused_computation.2 | custom fusion | bytes 8389120 | tf_op jit(solution)/shard_map/gather | solution.py:36
  110.5 4.8 %convolution_bitcast_fusion.1 = f32[128,16,128]{0,2,1:T(8,128)S(1)} fusion(bf16[16,8,128,128]{3,2,1,0:T(8,128)(2,1)} %bitcast.76, bf16[128,16,8,128]{3,0,2,1:T(8,128)(2,1)} %bitcast.78), kind=kOutput, calls=%fused_computation.14 | convolution fusion | flops 536870912 | bytes 9437184 | tf_op jit(solution)/shard_map/thkb,hkbc->thc/dot_general | solution.py:64
  115.3 31.9 %all-gather.4.cloned.1.call-done = bf16[128,128,128]{2,1,0:T(8,128)(2,1)} async-done(((bf16[8,128,128]{2,1,0:T(8,128)(2,1)}), bf16[128,128,128]{2,1,0:T(8,128)(2,1)}) %all-gather.4.cloned.1.call-update) | async-done | bytes 4194320 | tf_op jit(solution)/shard_map/all_gather | solution.py:69
  147.2 5.2 %gather_fusion.1 = bf16[128,128,128]{2,1,0:T(8,128)(2,1)} fusion(bf16[128,128,128]{2,1,0:T(8,128)(2,1)} %all-gather.4.cloned.1.call-done, s32[1024]{0:T(1024)S(1)} %pad_clamp_fusion.5), kind=kCustom, calls=%fused_computation.1 | custom fusion | bytes 8389120 | tf_op jit(solution)/shard_map/gather | solution.py:36
  152.5 5.0 %fusion.2 = bf16[128,16,128,1]{0,2,3,1:T(8,128)(2,1)S(1)} fusion(bf16[16,8,128,128]{3,2,1,0:T(8,128)(2,1)} %bitcast.84, bf16[128,16,8,128]{3,0,2,1:T(8,128)(2,1)} %bitcast.86, f32[128,16,128]{0,2,1:T(8,128)S(1)} %convolution_bitcast_fusion.1), kind=kOutput, calls=%fused_computation.17 | convolution fusion | flops 539492352 | bytes 9961472 | tf_op jit(solution)/shard_map/thkc,hkbc->thb/dot_general | solution.py:80
  157.4 3.3 convolution_convert_fusion.1
  160.8 5.2 %gather_fusion.6 = bf16[128,128,128]{2,1,0:T(8,128)(2,1)} fusion(bf16[128,128,128]{2,1,0:T(8,128)(2,1)} %bitcast.88, s32[1024]{0:T(1024)S(1)} %get-tuple-element.27), kind=kCustom, calls=%fused_computation.6 | custom fusion | bytes 8389120 | tf_op jit(solution)/shard_map/gather | solution.py:99
  166.0 0.0 reduce-scatter.11.cloned.1.call-start
  166.0 5.6 %convolution_convert_fusion = bf16[16,8,128,128]{3,2,1,0:T(8,128)(2,1)} fusion(bf16[128,16,8,128]{3,0,2,1:T(8,128)(2,1)} %bitcast.87, f32[128,16,128]{0,2,1:T(8,128)S(1)} %convolution_bitcast_fusion.1), kind=kOutput, calls=%fused_computation.10 | convolution fusion | flops 540278784 | bytes 9437184 | tf_op jit(solution)/shard_map/thb,thkc->hkbc/dot_general | solution.py:94
  171.7 6.4 %copy.79 = bf16[128,128,128]{2,1,0:T(8,128)(2,1)} copy(bf16[128,128,128]{1,2,0:T(8,128)(2,1)} %bitcast.89) | data formatting | bytes 8388608 | tf_op jit(solution)/shard_map/reshape | solution.py:98
  178.0 5.2 %gather_fusion.7 = bf16[128,128,128]{2,1,0:T(8,128)(2,1)} fusion(bf16[128,128,128]{2,1,0:T(8,128)(2,1)} %copy.79, s32[1024]{0:T(1024)S(1)} %get-tuple-element.26), kind=kCustom, calls=%fused_computation.7 | custom fusion | bytes 8389120 | tf_op jit(solution)/shard_map/gather | solution.py:100
  183.3 0.3 reduce-scatter.7.cloned.1.call-start
  183.6 6.7 %fusion.13 = f32[16,8,128,128]{3,2,1,0:T(8,128)} fusion(bf16[16,8,128,128]{3,2,1,0:T(8,128)(2,1)} %bitcast.77, bf16[128,16,128,1]{0,2,3,1:T(8,128)(2,1)S(1)} %fusion.2), kind=kOutput, calls=%fused_computation.57 | convolution fusion | flops 536870912 | bytes 13107200 | tf_op jit(solution)/shard_map/thc,hkbc->thkb/dot_general | solution.py:84
  190.3 9.0 %copy.73 = f32[128,128,128]{2,0,1:T(8,128)} copy(f32[128,128,128]{0,2,1:T(8,128)} %bitcast.82) | data formatting | bytes 16777216 | tf_op jit(solution)/shard_map/reshape | solution.py:27
  199.3 2.5 broadcast.43.clone.1
  201.8 26.7 %scatter_fusion.1 = f32[128,64,128]{2,0,1:T(8,128)} fusion(f32[128,64,128]{2,0,1:T(8,128)} %broadcast.43.clone.1, s32[128]{0:T(128)S(1)} %fusion.9, f32[128,128,128]{2,1,0:T(8,128)} %bitcast.81), kind=kCustom, calls=%fused_computation.9 | custom fusion | flops 2097152 | bytes 25166336 | tf_op jit(solution)/shard_map/scatter-add | solution.py:29
  228.5 2.6 convert_element_type.45
  231.1 2.9 copy.74
  234.1 0.0 reduce-scatter.5.cloned.1.call-start
  234.1 6.8 %fusion.11 = f32[16,8,128,128]{3,2,1,0:T(8,128)} fusion(bf16[16,8,128,128]{3,2,1,0:T(8,128)(2,1)} %bitcast.85, f32[128,16,128]{0,2,1:T(8,128)S(1)} %convolution_bitcast_fusion.1), kind=kOutput, calls=%fused_computation.56 | convolution fusion | flops 538181632 | bytes 13631488 | tf_op jit(solution)/shard_map/thb,hkbc->thkc/dot_general | solution.py:71
  240.9 9.0 %copy.68 = f32[128,128,128]{2,0,1:T(8,128)} copy(f32[128,128,128]{0,2,1:T(8,128)} %bitcast.83) | data formatting | bytes 16777216 | tf_op jit(solution)/shard_map/reshape | solution.py:27
  249.9 2.5 broadcast.43.clone
  252.4 26.9 %scatter_fusion = f32[128,64,128]{2,0,1:T(8,128)} fusion(f32[128,64,128]{2,0,1:T(8,128)} %broadcast.43.clone, s32[128]{0:T(128)S(1)} %fusion.8, f32[128,128,128]{2,1,0:T(8,128)} %bitcast.80), kind=kCustom, calls=%fused_computation.8 | custom fusion | flops 2097152 | bytes 25166336 | tf_op jit(solution)/shard_map/scatter-add | solution.py:29
  279.3 2.6 convert_element_type.42
  281.9 2.9 copy.69
  284.9 0.0 all-reduce.3.cloned.1.call-start
  284.9 0.0 reduce-scatter.9.cloned.1.call-done
  284.9 18.9 %reduce-scatter.11.cloned.1.call-done = bf16[8,128,128]{2,1,0:T(8,128)(2,1)} async-done(((bf16[128,128,128]{2,1,0:T(8,128)(2,1)}), bf16[8,128,128]{2,1,0:T(8,128)(2,1)}) %reduce-scatter.11.cloned.1.call-update) | async-done | bytes 262160 | tf_op jit(solution)/shard_map/reduce_scatter | solution.py:105
  303.9 42.0 %reduce-scatter.7.cloned.1.call-done = bf16[128,1024]{0,1:T(8,128)(2,1)} async-done(((bf16[128,8192]{0,1:T(8,128)(2,1)}), bf16[128,1024]{0,1:T(8,128)(2,1)}) %reduce-scatter.7.cloned.1.call-update) | async-done | bytes 262160 | tf_op jit(solution)/shard_map/reduce_scatter | solution.py:88
  345.9 1.8 copy.81
  347.7 41.8 %reduce-scatter.5.cloned.1.call-done = bf16[128,1024]{0,1:T(8,128)(2,1)} async-done(((bf16[128,8192]{0,1:T(8,128)(2,1)}), bf16[128,1024]{0,1:T(8,128)(2,1)}) %reduce-scatter.5.cloned.1.call-update) | async-done | bytes 262160 | tf_op jit(solution)/shard_map/reduce_scatter | solution.py:75
  389.5 1.8 copy.80
  391.3 45.9 %all-reduce.3.cloned.1.call-done = (bf16[8,128,128]{2,1,0:T(8,128)(2,1)}, bf16[8,128,128]{2,1,0:T(8,128)(2,1)}) async-done(((bf16[8,128,128]{2,1,0:T(8,128)(2,1)}, bf16[8,128,128]{2,1,0:T(8,128)(2,1)}), (bf16[8,128,128]{2,1,0:T(8,128)(2,1)}, bf16[8,128,128]{2,1,0:T(8,128)(2,1)})) %all-reduce.3.cloned.1.call-update) | async-done | bytes 524304 | tf_op jit(solution)/shard_map/psum | solution.py:110
  437.2 1.8 convert_element_type.48
  439.0 1.8 convert_element_type.51
  (49 shorter events, 0.8 us)
Async XLA Ops:
  7.2 14.3 %copy-start = (s32[128,1]{0,1:T(1,128)S(1)}, s32[128,1]{0,1:T(1,128)}, u32[]{:S(2)}) copy-start(s32[128,1]{0,1:T(1,128)} %param.12) | copy-start | bytes 1540
  7.2 64.4 %all-gather.8.cloned.1.call-start = ((), (), s32[]{:S(2)}) async-start(), calls=%async_computation.7 | async-start | bytes 2359296 | tf_op jit(solution)/shard_map/all_gather | solution.py:78
  9.0 96.3 %all-gather.6.cloned.1.call-start = ((), (), s32[]{:S(2)}) async-start(), calls=%async_computation.5 | async-start | bytes 4456448 | tf_op jit(solution)/shard_map/all_gather | solution.py:62
  9.8 137.4 %all-gather.4.cloned.1.call-start = ((), (), s32[]{:S(2)}) async-start(), calls=%async_computation.4 | async-start | bytes 4456448 | tf_op jit(solution)/shard_map/all_gather | solution.py:69
  10.5 274.4 %reduce-scatter.9.cloned.1.call-start = ((), (), s32[]{:S(2)}) async-start(), calls=%async_computation.9 | async-start | bytes 4456448 | tf_op jit(solution)/shard_map/reduce_scatter | solution.py:102
  11.7 14.2 %collective-permute-start = (bf16[128,1024]{0,1:T(8,128)(2,1)S(1)}, bf16[128,1024]{0,1:T(8,128)(2,1)S(1)}, u32[]{:S(2)}, u32[]{:S(2)}) collective-permute-start(bf16[128,1024]{0,1:T(8,128)(2,1)S(1)} %copy.60), channel_id=1, source_target_pairs={{0,1},{1,2},{2,3},{3,4},{4,5},{5,6},{6,7},{7,0},{8,9},{9,10},{10,1... | collective-permute-start | bytes 786440 | tf_op jit(solution)/shard_map/ppermute | solution.py:54
  14.2 24.8 %collective-permute-start.4 = (bf16[128,1024]{0,1:T(8,128)(2,1)S(1)}, bf16[128,1024]{0,1:T(8,128)(2,1)S(1)}, u32[]{:S(2)}, u32[]{:S(2)}) collective-permute-start(bf16[128,1024]{0,1:T(8,128)(2,1)S(1)} %copy.60), channel_id=1, source_target_pairs={{0,7},{1,0},{2,1},{3,2},{4,3},{5,4},{6,5},{7,6},{8,15},{9,8},{10,9... | collective-permute-start | bytes 786440 | tf_op jit(solution)/shard_map/ppermute | solution.py:56
  25.9 10.6 %collective-permute-start.1 = (bf16[128,1024]{0,1:T(8,128)(2,1)S(1)}, bf16[128,1024]{0,1:T(8,128)(2,1)S(1)}, u32[]{:S(2)}, u32[]{:S(2)}) collective-permute-start(bf16[128,1024]{0,1:T(8,128)(2,1)S(1)} %collective-permute-done), channel_id=1, source_target_pairs={{0,1},{1,2},{2,3},{3,4},{4,5},{5,6},{6,7},{7,0},{8,9},{9,10},{10,1... | collective-permute-start | bytes 786440 | tf_op jit(solution)/shard_map/ppermute | solution.py:54
  36.5 13.1 %collective-permute-start.2 = (bf16[128,1024]{0,1:T(8,128)(2,1)S(1)}, bf16[128,1024]{0,1:T(8,128)(2,1)S(1)}, u32[]{:S(2)}, u32[]{:S(2)}) collective-permute-start(bf16[128,1024]{0,1:T(8,128)(2,1)S(1)} %collective-permute-done.1), channel_id=1, source_target_pairs={{0,1},{1,2},{2,3},{3,4},{4,5},{5,6},{6,7},{7,0},{8,9},{9,10},{10,1... | collective-permute-start | bytes 786440 | tf_op jit(solution)/shard_map/ppermute | solution.py:54
  39.1 11.3 %collective-permute-start.5 = (bf16[128,1024]{0,1:T(8,128)(2,1)S(1)}, bf16[128,1024]{0,1:T(8,128)(2,1)S(1)}, u32[]{:S(2)}, u32[]{:S(2)}) collective-permute-start(bf16[128,1024]{0,1:T(8,128)(2,1)S(1)} %collective-permute-done.4), channel_id=1, source_target_pairs={{0,7},{1,0},{2,1},{3,2},{4,3},{5,4},{6,5},{7,6},{8,15},{9,8},{10,9... | collective-permute-start | bytes 786440 | tf_op jit(solution)/shard_map/ppermute | solution.py:56
  49.7 13.5 %collective-permute-start.3 = (bf16[128,1024]{0,1:T(8,128)(2,1)S(1)}, bf16[128,1024]{0,1:T(8,128)(2,1)S(1)}, u32[]{:S(2)}, u32[]{:S(2)}) collective-permute-start(bf16[128,1024]{0,1:T(8,128)(2,1)S(1)} %collective-permute-done.2), channel_id=1, source_target_pairs={{0,1},{1,2},{2,3},{3,4},{4,5},{5,6},{6,7},{7,0},{8,9},{9,10},{10,1... | collective-permute-start | bytes 786440 | tf_op jit(solution)/shard_map/ppermute | solution.py:54
  50.4 13.2 %collective-permute-start.6 = (bf16[128,1024]{0,1:T(8,128)(2,1)S(1)}, bf16[128,1024]{0,1:T(8,128)(2,1)S(1)}, u32[]{:S(2)}, u32[]{:S(2)}) collective-permute-start(bf16[128,1024]{0,1:T(8,128)(2,1)S(1)} %collective-permute-done.5), channel_id=1, source_target_pairs={{0,7},{1,0},{2,1},{3,2},{4,3},{5,4},{6,5},{7,6},{8,15},{9,8},{10,9... | collective-permute-start | bytes 786440 | tf_op jit(solution)/shard_map/ppermute | solution.py:56
  152.5 5.0 %copy-start.2 = (bf16[128,128,128]{2,1,0:T(8,128)(2,1)S(1)}, bf16[128,128,128]{2,1,0:T(8,128)(2,1)}, u32[]{:S(2)}) copy-start(bf16[128,128,128]{2,1,0:T(8,128)(2,1)} %gather_fusion.4) | copy-start | bytes 12582916
  166.0 137.9 %reduce-scatter.11.cloned.1.call-start = ((), (), s32[]{:S(2)}) async-start(), calls=%async_computation.10 | async-start | bytes 4456448 | tf_op jit(solution)/shard_map/reduce_scatter | solution.py:105
  183.3 162.6 %reduce-scatter.7.cloned.1.call-start = ((), (), s32[]{:S(2)}) async-start(), calls=%async_computation.8 | async-start | bytes 2359296 | tf_op jit(solution)/shard_map/reduce_scatter | solution.py:88
  234.1 155.4 %reduce-scatter.5.cloned.1.call-start = ((), (), s32[]{:S(2)}) async-start(), calls=%async_computation.6 | async-start | bytes 2359296 | tf_op jit(solution)/shard_map/reduce_scatter | solution.py:75
  279.3 161.5 %copy-start.1 = (s32[128,1]{0,1:T(1,128)S(1)}, s32[128,1]{0,1:T(1,128)}, u32[]{:S(2)}) copy-start(s32[128,1]{0,1:T(1,128)} %param.12) | copy-start | bytes 1540
  284.9 152.3 %all-reduce.3.cloned.1.call-start = ((), (), s32[]{:S(2)}) async-start(), calls=%async_computation.11 | async-start | bytes 1048576 | tf_op jit(solution)/shard_map/psum | solution.py:110
Sparse Core Ops, SparseCore 0:
  10.4 54.4 all-gather.7
  66.7 38.6 all-gather.5
  107.2 39.9 all-gather.3
  166.1 66.5 reduce-scatter.8
  235.2 68.6 reduce-scatter.10
  306.3 39.5 reduce-scatter.6
  348.4 40.9 reduce-scatter.4
  392.1 45.0 all-reduce.2
